TPU v7x, 256 devices: a whole 4x4x8 slice. The times are simulated.
256 devices in a mesh: node: 32 (over z_hi, x, core), ctrl: 8 (over y, z_lo).
Axes of the slice: x: 4, y: 4, z: 8 (z_hi: 4, z_lo: 2; z = z_hi * 2 + z_lo), core: 2. Of those that a mesh axis runs over, the one named last changes fastest.
Arguments:
- sensitivity: bfloat16 [96, 131072], P(None, 'node'), may hold values from -1 to 1
- node_xyz: float32 [3, 131072], P(None, 'node'), may hold values from 0 to 1
- ctrl_xyz: float32 [3, 16384], P(None, 'ctrl'), may hold values from 0 to 1
- inverse: bfloat16 [16384, 16384], P('ctrl', 'node'), may hold values from -0.046875 to 0.046875
Outputs:
- control_grad: float32 [96, 16384], P(None, ('node', 'ctrl'))
All inputs are finite; a program needn't handle non-finite values.
Results may differ from a plain program's by a relative error of at most 0.004.
Values may be sent and summed in bfloat16 or wider, within the bound.
No kernel may reach another device: no remote copies, remote signals or barrier semaphores. Data moves between devices by JAX's collectives and lax.ppermute only.
A program may use at most 64 MiB of HBM per device.

v0:
```python
import jax
import jax.numpy as jnp
from jax import lax
from jax.sharding import PartitionSpec as P

support_radius = 0.12


def cut_along(shard, dim, size):
    dims = shard.shape
    blocks = shard.reshape(*dims[:dim], size, dims[dim] // size, *dims[dim + 1 :])
    return jnp.moveaxis(blocks, dim, 0)


def sent_and_summed(shard, axis, dim):
    blocks = cut_along(shard, dim, lax.axis_size(axis))
    arrived = lax.all_to_all(blocks, axis, split_axis=0, concat_axis=0, tiled=True)
    return arrived.sum(axis=0)


def sent_to_all(shard, axis):
    copies = jnp.broadcast_to(shard, (lax.axis_size(axis), *shard.shape))
    return lax.all_to_all(copies, axis, split_axis=0, concat_axis=0, tiled=True)


def in_order(blocks, dim):
    dims = list(blocks.shape[1:])
    dims[dim] *= blocks.shape[0]
    return jnp.moveaxis(blocks, 0, dim).reshape(dims)


def gathered_copies(shard, axis, dim):
    blocks = sent_to_all(shard, axis)
    return in_order(blocks, dim)


def kernel_tile(node_part, ctrl_xyz):
    delta_x = node_part[0][:, None] - ctrl_xyz[0][None, :]
    delta_y = node_part[1][:, None] - ctrl_xyz[1][None, :]
    delta_z = node_part[2][:, None] - ctrl_xyz[2][None, :]
    scaled = jnp.sqrt(delta_x * delta_x + delta_y * delta_y + delta_z * delta_z) / support_radius
    remain = jnp.maximum(1.0 - scaled, 0.0)
    return (remain**4 * (4.0 * scaled + 1.0)).astype(jnp.bfloat16)


def per_device(sensitivity, node_xyz, ctrl_xyz, inverse):
    nodes_here = node_xyz.shape[1]
    span_rows = min(1024, nodes_here)
    steps_count = nodes_here // span_rows

    def advance(number, running):
        offset = number * span_rows
        node_part = lax.dynamic_slice_in_dim(node_xyz, offset, span_rows, 1)
        sens_part = lax.dynamic_slice_in_dim(sensitivity, offset, span_rows, 1)
        weights_tile = kernel_tile(node_part, ctrl_xyz)
        return running + jnp.dot(sens_part, weights_tile, preferred_element_type=jnp.float32)

    start_sum = jnp.zeros((sensitivity.shape[0], ctrl_xyz.shape[1]), jnp.float32)
    partial_pull = lax.fori_loop(0, steps_count, advance, start_sum)
    share_low = sent_and_summed(partial_pull, "node", 1).astype(jnp.bfloat16)
    product = jnp.dot(
        gathered_copies(share_low, "node", 1), inverse, preferred_element_type=jnp.float32
    )
    return sent_and_summed(product, "ctrl", 1)


def solution(mesh):
    in_specs = (P(None, "node"), P(None, "node"), P(None, "ctrl"), P("ctrl", "node"))
    out_specs = P(None, ("node", "ctrl"))
    return jax.shard_map(
        per_device, mesh=mesh, in_specs=in_specs, out_specs=out_specs, check_vma=False
    )
```

profile of v0, /device:TPU:1, one launch (start us, length us, event | category | flops | bytes accessed | tf_op | source)
XLA Modules:
  0.0 117.3 jit_solution(4098370373425946439)
XLA Ops:
  0.0 38.3 %while.16 = (s32[]{:T(128)}, f32[96,2048]{1,0:T(8,128)S(1)}, bf16[96,4096]{1,0:T(8,128)(2,1)}, f32[3,4096]{1,0:T(4,128)}, f32[3,2048]{1,0:T(4,128)}, /*index=5*/...) while((s32[]{:T(128)}, f32[96,2048]{1,0:T(8,128)S(1)}, ...), condition=%wide.region_1.0_spmd.clone, body=%wide.region_0.0_spmd.clone.sunk | while | flops 438697984 | bytes 1880277 | solution.py:59
  0.0 0.9 constant_dynamic-slice_fusion.2
  0.9 0.9 fusion.15
  1.8 7.7 %fusion.16 = f32[96,2048]{1,0:T(8,128)S(1)} fusion(f32[2048]{0:T(1024)S(1)} %bitcast.37, f32[1024]{0:T(1024)S(1)} %bitcast.41, f32[2048]{0:T(1024)S(1)} %bitcast.38, f32[1024]{0:T(1024)S(1)} %bitcast.40, f32[2048]{0:T(1024)S(1)} %bitcast.36, f32[1024]{0:T(1024)S(1)} %bitcast.39, f32[96,2048]{1,0:T(8,128)S(1)} %get-tuple-element.227, ...), kind=kOutput, calls=%fused_computation.2.clone.1 | convolution fusion | flops 438697984 | bytes 1806341 | tf_op jit(solution)/shard_map/while/body/eval_jaxpr/dot_general | solution.py:56
  9.6 0.9 constant_dynamic-slice_fusion.2
  10.5 0.9 fusion.15
  11.4 7.7 %fusion.16 = f32[96,2048]{1,0:T(8,128)S(1)} fusion(f32[2048]{0:T(1024)S(1)} %bitcast.37, f32[1024]{0:T(1024)S(1)} %bitcast.41, f32[2048]{0:T(1024)S(1)} %bitcast.38, f32[1024]{0:T(1024)S(1)} %bitcast.40, f32[2048]{0:T(1024)S(1)} %bitcast.36, f32[1024]{0:T(1024)S(1)} %bitcast.39, f32[96,2048]{1,0:T(8,128)S(1)} %get-tuple-element.227, ...), kind=kOutput, calls=%fused_computation.2.clone.1 | convolution fusion | flops 438697984 | bytes 1806341 | tf_op jit(solution)/shard_map/while/body/eval_jaxpr/dot_general | solution.py:56
  19.2 0.9 constant_dynamic-slice_fusion.2
  20.1 0.9 fusion.15
  21.0 7.7 %fusion.16 = f32[96,2048]{1,0:T(8,128)S(1)} fusion(f32[2048]{0:T(1024)S(1)} %bitcast.37, f32[1024]{0:T(1024)S(1)} %bitcast.41, f32[2048]{0:T(1024)S(1)} %bitcast.38, f32[1024]{0:T(1024)S(1)} %bitcast.40, f32[2048]{0:T(1024)S(1)} %bitcast.36, f32[1024]{0:T(1024)S(1)} %bitcast.39, f32[96,2048]{1,0:T(8,128)S(1)} %get-tuple-element.227, ...), kind=kOutput, calls=%fused_computation.2.clone.1 | convolution fusion | flops 438697984 | bytes 1806341 | tf_op jit(solution)/shard_map/while/body/eval_jaxpr/dot_general | solution.py:56
  28.7 0.9 constant_dynamic-slice_fusion.2
  29.7 0.9 fusion.15
  30.6 7.7 %fusion.16 = f32[96,2048]{1,0:T(8,128)S(1)} fusion(f32[2048]{0:T(1024)S(1)} %bitcast.37, f32[1024]{0:T(1024)S(1)} %bitcast.41, f32[2048]{0:T(1024)S(1)} %bitcast.38, f32[1024]{0:T(1024)S(1)} %bitcast.40, f32[2048]{0:T(1024)S(1)} %bitcast.36, f32[1024]{0:T(1024)S(1)} %bitcast.39, f32[96,2048]{1,0:T(8,128)S(1)} %get-tuple-element.227, ...), kind=kOutput, calls=%fused_computation.2.clone.1 | convolution fusion | flops 438697984 | bytes 1806341 | tf_op jit(solution)/shard_map/while/body/eval_jaxpr/dot_general | solution.py:56
  38.3 0.3 copy.6
  38.6 39.9 %all_to_all.15 = f32[32,96,64]{1,2,0:T(8,128)S(1)} all-to-all(f32[32,96,64]{1,2,0:T(8,128)S(1)} %bitcast.34), channel_id=1, replica_groups=mesh['node'=32,'ctrl'=8] {'node'}, dimensions={0} | all-to-all | bytes 1572864 | tf_op jit(solution)/shard_map/all_to_all | solution.py:17
  78.6 0.1 reduce_sum.18
  78.7 0.9 broadcast_in_dim.7
  79.6 6.5 %all-to-all-start.1 = ((bf16[32,96,64]{1,2,0:T(8,128)(2,1)}), bf16[32,96,64]{1,2,0:T(8,128)(2,1)S(1)}, u32[]{:S(2)}, u32[]{:S(2)}) async-start(bf16[32,96,64]{1,2,0:T(8,128)(2,1)} %broadcast_in_dim.7), calls=%async_computation.1 | async-start | bytes 1048576 | tf_op jit(solution)/shard_map/all_to_all | solution.py:23
  86.1 2.9 %copy.7 = bf16[2048,512]{0,1:T(8,128)(2,1)S(1)} copy(bf16[2048,512]{1,0:T(8,128)(2,1)} %param.9) | data formatting | bytes 4194304 | tf_op args[3]
  89.1 15.2 %all-to-all-done.1 = bf16[32,96,64]{1,2,0:T(8,128)(2,1)S(1)} async-done(((bf16[32,96,64]{1,2,0:T(8,128)(2,1)}), bf16[32,96,64]{1,2,0:T(8,128)(2,1)S(1)}, u32[]{:S(2)}, u32[]{:S(2)}) %all-to-all-start.1) | async-done | bytes 393248 | tf_op jit(solution)/shard_map/all_to_all | solution.py:23
  104.3 0.7 convolution_bitcast_fusion
  105.0 11.7 %all_to_all.16 = f32[8,96,64]{1,2,0:T(8,128)S(1)} all-to-all(f32[8,96,64]{1,2,0:T(8,128)S(1)} %convolution_bitcast_fusion), channel_id=1, replica_groups=mesh['node'=32,'ctrl'=8] {'ctrl'}, dimensions={0} | all-to-all | bytes 393216 | tf_op jit(solution)/shard_map/all_to_all | solution.py:17
  116.7 0.6 reduce_sum.19
  (1 shorter events, 0.0 us)
Async XLA Ops:
  79.6 24.7 %all-to-all-start.1 = ((bf16[32,96,64]{1,2,0:T(8,128)(2,1)}), bf16[32,96,64]{1,2,0:T(8,128)(2,1)S(1)}, u32[]{:S(2)}, u32[]{:S(2)}) async-start(bf16[32,96,64]{1,2,0:T(8,128)(2,1)} %broadcast_in_dim.7), calls=%async_computation.1 | async-start | bytes 1048576 | tf_op jit(solution)/shard_map/all_to_all | solution.py:23
where the time goes:
time: 118 us; the launch traced here: 117 us
  blocking collectives  51.6 us (44%)
  matrix products  31.6 us (27%)
  waiting for transfers between devices  15.2 us (13%)
  local copies, waits for them, and re-layouts  11.4 us (10%)
  starting transfers between devices  6.53 us (6%)
    all_to_all x2, blocking collectives, sent_and_summed(): lax.all_to_all(blocks, axis, split_axis=0, concat_axis=0, tiled=True)  51.6 us
    dot_general x4, matrix products, advance(): jnp.dot(sens_part, weights_tile, preferred_element_type=jnp.float32)  30.9 us
    all_to_all x1, waiting for transfers between devices, sent_to_all(): return lax.all_to_all(copies, axis, split_axis=0, concat_axis=0, tiled=True)  15.2 us
    slice x8, local copies, waits for them, and re-layouts, kernel_tile(): delta_x = node_part[0][:, None] - ctrl_xyz[0][None, :]  7.27 us
    all_to_all x1, starting transfers between devices, sent_to_all(): return lax.all_to_all(copies, axis, split_axis=0, concat_axis=0, tiled=True)  6.53 us
    unnamed x1, local copies, waits for them, and re-layouts  2.93 us
  transfers between devices with their start and end apart: 1, of which 1 were waited for; matrix products, arithmetic and copies ran while one was open for 3% of the time, Pallas kernels for 0%

commit v1 on v0

v1 whole, which is shorter than its diff:
```python
import functools

import jax
import jax.numpy as jnp
from jax import lax
from jax.experimental import pallas as pl
from jax.experimental.pallas import tpu as pltpu
from jax.sharding import Mesh, PartitionSpec as P

support_radius = 0.12
stretch = 4.0 / support_radius
depth = 128
span = 256


def pieces_of(values):
    high = values.astype(jnp.bfloat16).astype(jnp.float32)
    rest = values - high
    middle = rest.astype(jnp.bfloat16).astype(jnp.float32)
    low = (rest - middle).astype(jnp.bfloat16).astype(jnp.float32)
    return high, middle, low


def write_features(xyz_ref, rows, is_node):
    count = xyz_ref.shape[1]
    place = (xyz_ref[...] - 0.5) * stretch
    norm = (
        place[0:1] * place[0:1] + place[1:2] * place[1:2] + place[2:3] * place[2:3]
    )
    parts = pieces_of(place)
    norm_parts = pieces_of(norm)
    ones = jnp.ones((3, count), jnp.float32)
    rows[...] = jnp.zeros_like(rows)
    for i in range(3):
        for j in range(3):
            k = 3 * (3 * i + j)
            rows[k : k + 3, :] = parts[i] if is_node else -2.0 * parts[j]
    norm_at, ones_at = (27, 30) if is_node else (30, 27)
    rows[ones_at : ones_at + 3, :] = ones
    for i in range(3):
        rows[norm_at + i : norm_at + i + 1, :] = norm_parts[i]


def features_kernel(node_ref, ctrl_ref, node_out, ctrl_out, node_rows, ctrl_rows):
    write_features(node_ref, node_rows, True)
    write_features(ctrl_ref, ctrl_rows, False)
    ctrl_out[...] = ctrl_rows[...].astype(jnp.bfloat16)
    node_out[...] = node_rows[...].T.astype(jnp.bfloat16)


def features(node_xyz, ctrl_xyz):
    nodes, ctrls = node_xyz.shape[1], ctrl_xyz.shape[1]
    return pl.pallas_call(
        features_kernel,
        out_shape=[
            jax.ShapeDtypeStruct((nodes, depth), jnp.bfloat16),
            jax.ShapeDtypeStruct((depth, ctrls), jnp.bfloat16),
        ],
        scratch_shapes=[
            pltpu.VMEM((depth, nodes), jnp.float32),
            pltpu.VMEM((depth, ctrls), jnp.float32),
        ],
        cost_estimate=pl.CostEstimate(
            flops=nodes * 1000, bytes_accessed=nodes * 512, transcendentals=0
        ),
        name="features",
    )(node_xyz, ctrl_xyz)


def wendland(squared):
    squared = jnp.maximum(squared, 1e-30)
    r4 = squared * lax.rsqrt(squared)
    remain = jnp.maximum(4.0 - r4, 0.0)
    remain2 = remain * remain
    return (remain2 * remain2 * (r4 + 1.0)).astype(jnp.bfloat16)


def pull_kernel(tile, has_add, index_ref, node_ref, ctrl_ref, sens_ref, *rest):
    out_ref = rest[-1]
    nodes = node_ref.shape[0]

    def body(i, acc):
        at = pl.multiple_of(i * tile, tile)
        squared = jnp.dot(
            node_ref[pl.ds(at, tile), :],
            ctrl_ref[...],
            preferred_element_type=jnp.float32,
        )
        return acc + jnp.dot(
            sens_ref[:, pl.ds(at, tile)],
            wendland(squared),
            preferred_element_type=jnp.float32,
        )

    acc = lax.fori_loop(0, nodes // tile, body, jnp.zeros(out_ref.shape, jnp.float32))
    acc = acc * (1.0 / 256.0)
    if has_add:
        acc = acc + rest[0][...]
    out_ref[...] = acc


def pull(index, blocks, node_feat, ctrl_feat, sens, add=None, tile=2048):
    nodes = node_feat.shape[0]
    rows = sens.shape[0]
    in_specs = [
        pl.BlockSpec((nodes, depth), lambda i, idx: (0, 0)),
        pl.BlockSpec((depth, span), lambda i, idx: (0, idx[i])),
        pl.BlockSpec((rows, nodes), lambda i, idx: (0, 0)),
    ]
    args = [node_feat, ctrl_feat, sens]
    if add is not None:
        in_specs.append(pl.BlockSpec((rows, span), lambda i, idx: (0, idx[blocks])))
        args.append(add)
    return pl.pallas_call(
        functools.partial(pull_kernel, tile, add is not None),
        out_shape=jax.ShapeDtypeStruct((rows, blocks * span), jnp.float32),
        grid_spec=pltpu.PrefetchScalarGridSpec(
            num_scalar_prefetch=1,
            grid=(blocks,),
            in_specs=in_specs,
            out_specs=pl.BlockSpec((rows, span), lambda i, idx: (0, i)),
        ),
        cost_estimate=pl.CostEstimate(
            flops=blocks * span * nodes * 400,
            bytes_accessed=nodes * 448,
            transcendentals=blocks * span * nodes,
        ),
        name="pull",
    )(index, *args)


def product_kernel(index_ref, *refs):
    blocks, inverse_ref, out_ref = refs[:-2], refs[-2], refs[-1]
    total = None
    for i, block in enumerate(blocks):
        half = block.shape[1]
        at = pl.multiple_of(index_ref[i] * half, half)
        term = jnp.dot(
            block[...],
            inverse_ref[pl.ds(at, half), :],
            preferred_element_type=jnp.float32,
        )
        total = term if total is None else total + term
    shares, rows, lanes = out_ref.shape
    width = lanes // 2
    for j in range(shares):
        share = total[:, j * width : (j + 1) * width]
        out_ref[j] = jnp.concatenate([share[:rows], share[rows:]], axis=1).astype(
            out_ref.dtype
        )


def product(index, blocks, inverse, shares):
    rows, width = blocks[0].shape[0], inverse.shape[1] // shares
    count = len(blocks)
    whole = pl.BlockSpec(memory_space=pltpu.VMEM)
    return pl.pallas_call(
        product_kernel,
        out_shape=jax.ShapeDtypeStruct((shares, rows // 2, 2 * width), jnp.bfloat16),
        in_specs=[pl.BlockSpec(memory_space=pltpu.SMEM)] + [whole] * (count + 1),
        out_specs=whole,
        name="product",
    )(index, *blocks, inverse)


def finish_kernel(shares_ref, out_ref):
    total = shares_ref[0].astype(jnp.float32)
    for j in range(1, shares_ref.shape[0]):
        total = total + shares_ref[j].astype(jnp.float32)
    rows, lanes = total.shape
    out_ref[0:rows, :] = total[:, : lanes // 2]
    out_ref[rows:, :] = total[:, lanes // 2 :]


def finish(shares):
    _, rows, lanes = shares.shape
    return pl.pallas_call(
        finish_kernel,
        out_shape=jax.ShapeDtypeStruct((2 * rows, lanes // 2), jnp.float32),
        name="finish",
    )(shares)


def shifted(value, axis, by):
    size = lax.axis_size(axis)
    return lax.ppermute(value, axis, [(i, (i + by) % size) for i in range(size)])


def per_device(sensitivity, node_xyz, ctrl_xyz, inverse):
    core = lax.axis_index("core").astype(jnp.int32)
    x = lax.axis_index("x").astype(jnp.int32)
    node_feat, ctrl_feat = features(node_xyz, ctrl_xyz)

    own = core * 4
    other = (1 - core) * 4
    other_index = other + jnp.arange(5, dtype=jnp.int32) % 4
    for_other = pull(other_index, 4, node_feat, ctrl_feat, sensitivity)
    from_other = shifted(for_other, "core", 1)

    def quarter(by, add):
        which = (x + by) % 4
        index = jnp.stack([own + which, which])
        return pull(index, 1, node_feat, ctrl_feat, sensitivity, add)

    arrived = []
    for by in (2, 1, 3):
        arrived.append(shifted(quarter(by, from_other), "x", by))
    summed = quarter(0, from_other) + arrived[0] + arrived[1] + arrived[2]

    low = summed.astype(jnp.bfloat16)
    for by in (2, 1, 3):
        summed = summed + shifted(low, "zh", by).astype(jnp.float32)
    mine = summed.astype(jnp.bfloat16)

    along_x = [mine] + [shifted(mine, "x", by) for by in (2, 1, 3)]
    index_x = [(x - by) % 4 for by in (0, 2, 1, 3)]
    joined = jnp.concatenate(along_x, axis=1)
    swapped = shifted(joined, "core", 1)
    both = [b for b in along_x] + [
        swapped[:, i * span : (i + 1) * span] for i in range(4)
    ]
    index = jnp.stack([own + i for i in index_x] + [other + i for i in index_x])
    shares = product(index, both, inverse, 8)
    arrived_shares = lax.all_to_all(
        shares, ("y", "zl"), split_axis=0, concat_axis=0, tiled=True
    )
    return finish(arrived_shares)


def solution(mesh):
    fine = Mesh(
        mesh.devices.reshape(4, 4, 2, 4, 2), ("zh", "x", "core", "y", "zl")
    )
    node, ctrl = ("zh", "x", "core"), ("y", "zl")
    in_specs = (P(None, node), P(None, node), P(None, ctrl), P(ctrl, node))
    out_specs = P(None, node + ctrl)
    return jax.shard_map(
        per_device, mesh=fine, in_specs=in_specs, out_specs=out_specs, check_vma=False
    )
```

time: 118 us -> 87.8 us (0.74)
  blocking collectives: 51.6 us -> 10.9 us
  Pallas kernels: 0 us -> 38.2 us
  matrix products: 31.6 us -> 0 us
  starting transfers between devices: 6.53 us -> 21.7 us
  local copies, waits for them, and re-layouts: 11.4 us -> 3.52 us
  waiting for transfers between devices: 15.2 us -> 8.93 us
  other arithmetic: 0.73 us -> 3.92 us
    all_to_all x2 -> x1, blocking collectives: 51.6 us -> 10.9 us  [per_device(): lax.all_to_all(shares, ('y', 'zl'), split_axis=0, concat_axis=0, tiled=True)]
    pallas_call x0 -> x8, Pallas kernels: none -> 38.2 us  [the longest x5 31.1 us: pull(): pl.pallas_call(functools.partial(pull_kernel, tile, add is not None), out...]
    dot_general x5 -> x0, matrix products: 31.6 us -> none  [the longest x4 30.9 us: advance(): jnp.dot(sens_part, weights_tile, preferred_element_type=jnp.float32)]
    ppermute x0 -> x11, starting transfers between devices: none -> 21.7 us  [shifted(): lax.ppermute(value, axis, [(i, (i + by) % size) for i in range(size)])]
    all_to_all x1 -> x0, waiting for transfers between devices: 15.2 us -> none  [sent_to_all(): return lax.all_to_all(copies, axis, split_axis=0, concat_axis=0, tiled=True)]
    ppermute x0 -> x11, waiting for transfers between devices: none -> 8.93 us  [shifted(): lax.ppermute(value, axis, [(i, (i + by) % size) for i in range(size)])]
    slice x8 -> x1, local copies, waits for them, and re-layouts: 7.27 us -> 0.68 us  [per_device(): swapped[:, i * span:(i + 1) * span]]
    all_to_all x1 -> x0, starting transfers between devices: 6.53 us -> none  [sent_to_all(): return lax.all_to_all(copies, axis, split_axis=0, concat_axis=0, tiled=True)]
  transfers between devices with their start and end apart: 1 -> 11, of which waited for: 1 -> 6; matrix products, arithmetic and copies ran while one was open for 3% -> 3% of each run, Pallas kernels for 0% -> 17%
where the time goes in v1:
time: 87.8 us; the launch traced here: 87.3 us
  Pallas kernels  38.2 us (44%)
  starting transfers between devices  21.7 us (25%)
  blocking collectives  10.9 us (12%)
  waiting for transfers between devices  8.93 us (10%)
  other arithmetic  3.92 us (4%)
  local copies, waits for them, and re-layouts  3.52 us (4%)
    pallas_call x5, Pallas kernels, pull(): pl.pallas_call(functools.partial(pull_kernel, tile, add is not None), out...  31.1 us
    ppermute x11, starting transfers between devices, shifted(): lax.ppermute(value, axis, [(i, (i + by) % size) for i in range(size)])  21.7 us
    all_to_all x1, blocking collectives, per_device(): lax.all_to_all(shares, ('y', 'zl'), split_axis=0, concat_axis=0, tiled=True)  10.9 us
    ppermute x11, waiting for transfers between devices, shifted(): lax.ppermute(value, axis, [(i, (i + by) % size) for i in range(size)])  8.93 us
    pallas_call x1, Pallas kernels, product(): pl.pallas_call(product_kernel, out_shape=jax.ShapeDtypeStruct((shares, ro...  3.04 us
    pallas_call x1, Pallas kernels, features(): pl.pallas_call(features_kernel, out_shape=[jax.ShapeDtypeStruct((nodes, d...  2.49 us
    another operation x4, other arithmetic, quarter(): index = jnp.stack([own + which, which])  2.45 us
  transfers between devices with their start and end apart: 11, of which 6 were waited for; matrix products, arithmetic and copies ran while one was open for 3% of the time, Pallas kernels for 17%

profile of v1, /device:TPU:1, one launch (start us, length us, event | category | flops | bytes accessed | tf_op | source)
XLA Modules:
  0.0 87.3 jit_solution(17278489842510814793)
XLA Ops:
  0.5 2.5 %features.1 = (bf16[4096,128]{1,0:T(8,128)(2,1)}, bf16[128,2048]{1,0:T(8,128)(2,1)}) custom-call(f32[3,4096]{1,0:T(4,128)} %node_ref.1, f32[3,2048]{1,0:T(4,128)} %ctrl_ref.1), custom_call_target="tpu_custom_call" | custom-call | flops 4096000 | bytes 2097152 | tf_op jit(solution)/shard_map/features/pallas_call | solution.py:53
  3.0 11.4 %pull.5 = f32[96,1024]{1,0:T(8,128)} custom-call(s32[5]{0:T(128)} %fusion.index_ref, bf16[4096,128]{1,0:T(8,128)(2,1)} %get-tuple-element.7.node_ref, bf16[128,2048]{1,0:T(8,128)(2,1)} %get-tuple-element.8.ctrl_ref, bf16[96,4096]{1,0:T(8,128)(2,1)} %sens_ref.9), custom_call_target="tpu_custom_call" | custom-call | flops 1677721600 | bytes 1835008 | tf_op jit(solution)/shard_map/pull/pallas_call | solution.py:114
  14.4 3.2 %collective-permute-start = (f32[96,1024]{1,0:T(8,128)}, f32[96,1024]{1,0:T(8,128)S(1)}, u32[]{:S(2)}, u32[]{:S(2)}) collective-permute-start(f32[96,1024]{1,0:T(8,128)} %pull.5), channel_id=1, source_target_pairs={{0,8},{8,0},{1,9},{9,1},{2,10},{10,2},{3,11},{11,3},{4,12},{12,4},... | collective-permute-start | bytes 1179656 | tf_op jit(solution)/shard_map/ppermute | solution.py:186
  19.4 0.8 copy-done
  20.2 4.9 %pull.7 = f32[96,256]{1,0:T(8,128)} custom-call(s32[2]{0:T(128)} %pad_add_fusion.1.index_ref, bf16[4096,128]{1,0:T(8,128)(2,1)} %get-tuple-element.7.node_ref, bf16[128,2048]{1,0:T(8,128)(2,1)} %get-tuple-element.8.ctrl_ref, bf16[96,4096]{1,0:T(8,128)(2,1)} %sens_ref.9, f32[96,1024]{1,0:T(8,128)} %copy-done), custom_call_target="tpu_custom_call" | custom-call | flops 419430400 | bytes 1835008 | tf_op jit(solution)/shard_map/pull/pallas_call | solution.py:114
  25.1 1.0 %collective-permute-start.1 = (f32[96,256]{1,0:T(8,128)}, f32[96,256]{1,0:T(8,128)S(1)}, u32[]{:S(2)}, u32[]{:S(2)}) collective-permute-start(f32[96,256]{1,0:T(8,128)} %pull.7), channel_id=1, source_target_pairs={{0,32},{16,48},{32,0},{48,16},{1,33},{17,49},{33,1},{49,17},{2,34}... | collective-permute-start | bytes 294920 | tf_op jit(solution)/shard_map/ppermute | solution.py:186
  26.2 4.9 %pull.8 = f32[96,256]{1,0:T(8,128)} custom-call(s32[2]{0:T(128)} %pad_add_fusion.2.index_ref, bf16[4096,128]{1,0:T(8,128)(2,1)} %get-tuple-element.7.node_ref, bf16[128,2048]{1,0:T(8,128)(2,1)} %get-tuple-element.8.ctrl_ref, bf16[96,4096]{1,0:T(8,128)(2,1)} %sens_ref.9, f32[96,1024]{1,0:T(8,128)} %copy-done), custom_call_target="tpu_custom_call" | custom-call | flops 419430400 | bytes 1835008 | tf_op jit(solution)/shard_map/pull/pallas_call | solution.py:114
  31.4 4.9 %pull.9 = f32[96,256]{1,0:T(8,128)} custom-call(s32[2]{0:T(128)} %pad_add_fusion.3.index_ref, bf16[4096,128]{1,0:T(8,128)(2,1)} %get-tuple-element.7.node_ref, bf16[128,2048]{1,0:T(8,128)(2,1)} %get-tuple-element.8.ctrl_ref, bf16[96,4096]{1,0:T(8,128)(2,1)} %sens_ref.9, f32[96,1024]{1,0:T(8,128)} %copy-done), custom_call_target="tpu_custom_call" | custom-call | flops 419430400 | bytes 1835008 | tf_op jit(solution)/shard_map/pull/pallas_call | solution.py:114
  36.3 2.4 %collective-permute-start.3 = (f32[96,256]{1,0:T(8,128)}, f32[96,256]{1,0:T(8,128)S(1)}, u32[]{:S(2)}, u32[]{:S(2)}) collective-permute-start(f32[96,256]{1,0:T(8,128)} %pull.9), channel_id=1, source_target_pairs={{0,48},{16,0},{32,16},{48,32},{1,49},{17,1},{33,17},{49,33},{2,50}... | collective-permute-start | bytes 294920 | tf_op jit(solution)/shard_map/ppermute | solution.py:186
  39.3 4.9 %pull.6 = f32[96,256]{1,0:T(8,128)} custom-call(s32[2]{0:T(128)} %pad_add_fusion.index_ref, bf16[4096,128]{1,0:T(8,128)(2,1)} %get-tuple-element.7.node_ref, bf16[128,2048]{1,0:T(8,128)(2,1)} %get-tuple-element.8.ctrl_ref, bf16[96,4096]{1,0:T(8,128)(2,1)} %sens_ref.9, f32[96,1024]{1,0:T(8,128)} %copy-done), custom_call_target="tpu_custom_call" | custom-call | flops 419430400 | bytes 1835008 | tf_op jit(solution)/shard_map/pull/pallas_call | solution.py:114
  44.3 0.9 %fusion.1 = (bf16[96,256]{1,0:T(8,128)(2,1)S(1)}, f32[96,256]{1,0:T(8,128)S(1)}) fusion(f32[96,256]{1,0:T(8,128)S(1)} %collective-permute-done.3, f32[96,256]{1,0:T(8,128)S(1)} %collective-permute-done.2, f32[96,256]{1,0:T(8,128)} %pull.6, f32[96,256]{1,0:T(8,128)S(1)} %collective-permute-done.1), kind=kLoop, calls=%fused_computation.9 | loop fusion | flops 98304 | bytes 540672 | tf_op jit(solution)/shard_map/convert_element_type | solution.py:210
  45.2 6.1 %collective-permute-start.6 = (bf16[96,256]{1,0:T(8,128)(2,1)S(1)}, bf16[96,256]{1,0:T(8,128)(2,1)S(1)}, u32[]{:S(2)}, u32[]{:S(2)}) collective-permute-start(bf16[96,256]{1,0:T(8,128)(2,1)S(1)} %get-tuple-element.9), channel_id=1, source_target_pairs={{0,192},{64,0},{128,64},{192,128},{1,193},{65,1},{129,65},{193,129... | collective-permute-start | bytes 147464 | tf_op jit(solution)/shard_map/ppermute | solution.py:186
  51.3 3.3 %collective-permute-start.4 = (bf16[96,256]{1,0:T(8,128)(2,1)S(1)}, bf16[96,256]{1,0:T(8,128)(2,1)S(1)}, u32[]{:S(2)}, u32[]{:S(2)}) collective-permute-start(bf16[96,256]{1,0:T(8,128)(2,1)S(1)} %get-tuple-element.9), channel_id=1, source_target_pairs={{0,128},{64,192},{128,0},{192,64},{1,129},{65,193},{129,1},{193,65... | collective-permute-start | bytes 147464 | tf_op jit(solution)/shard_map/ppermute | solution.py:186
  54.6 1.9 %collective-permute-done.5 = bf16[96,256]{1,0:T(8,128)(2,1)S(1)} collective-permute-done((bf16[96,256]{1,0:T(8,128)(2,1)S(1)}, bf16[96,256]{1,0:T(8,128)(2,1)S(1)}, u32[]{:S(2)}, u32[]{:S(2)}) %collective-permute-start.5) | collective-permute-done | bytes 49184 | tf_op jit(solution)/shard_map/ppermute | solution.py:186
  56.4 1.9 %collective-permute-done.4 = bf16[96,256]{1,0:T(8,128)(2,1)S(1)} collective-permute-done((bf16[96,256]{1,0:T(8,128)(2,1)S(1)}, bf16[96,256]{1,0:T(8,128)(2,1)S(1)}, u32[]{:S(2)}, u32[]{:S(2)}) %collective-permute-start.4) | collective-permute-done | bytes 49184 | tf_op jit(solution)/shard_map/ppermute | solution.py:186
  58.6 1.3 %collective-permute-start.8 = (bf16[96,256]{1,0:T(8,128)(2,1)S(1)}, bf16[96,256]{1,0:T(8,128)(2,1)S(1)}, u32[]{:S(2)}, u32[]{:S(2)}) collective-permute-start(bf16[96,256]{1,0:T(8,128)(2,1)S(1)} %add_convert_fusion.refs_0_), channel_id=1, source_target_pairs={{0,16},{16,32},{32,48},{48,0},{1,17},{17,33},{33,49},{49,1},{2,18}... | collective-permute-start | bytes 147464 | tf_op jit(solution)/shard_map/ppermute | solution.py:186
  59.9 1.5 %collective-permute-done.9.refs_3_ = bf16[96,256]{1,0:T(8,128)(2,1)S(1)} collective-permute-done((bf16[96,256]{1,0:T(8,128)(2,1)S(1)}, bf16[96,256]{1,0:T(8,128)(2,1)S(1)}, u32[]{:S(2)}, u32[]{:S(2)}) %collective-permute-start.9) | collective-permute-done | bytes 49184 | tf_op jit(solution)/shard_map/ppermute | solution.py:186
  61.4 1.4 %collective-permute-done.8.refs_2_ = bf16[96,256]{1,0:T(8,128)(2,1)S(1)} collective-permute-done((bf16[96,256]{1,0:T(8,128)(2,1)S(1)}, bf16[96,256]{1,0:T(8,128)(2,1)S(1)}, u32[]{:S(2)}, u32[]{:S(2)}) %collective-permute-start.8) | collective-permute-done | bytes 49184 | tf_op jit(solution)/shard_map/ppermute | solution.py:186
  62.8 1.8 %collective-permute-done.7.refs_1_ = bf16[96,256]{1,0:T(8,128)(2,1)S(1)} collective-permute-done((bf16[96,256]{1,0:T(8,128)(2,1)S(1)}, bf16[96,256]{1,0:T(8,128)(2,1)S(1)}, u32[]{:S(2)}, u32[]{:S(2)}) %collective-permute-start.7) | collective-permute-done | bytes 49184 | tf_op jit(solution)/shard_map/ppermute | solution.py:186
  64.6 3.9 %collective-permute-start.10 = (bf16[96,1024]{1,0:T(8,128)(2,1)S(1)}, bf16[96,1024]{1,0:T(8,128)(2,1)S(1)}, u32[]{:S(2)}, u32[]{:S(2)}) collective-permute-start(bf16[96,1024]{1,0:T(8,128)(2,1)S(1)} %pad_maximum_fusion), channel_id=1, source_target_pairs={{0,8},{8,0},{1,9},{9,1},{2,10},{10,2},{3,11},{11,3},{4,12},{12,4},... | collective-permute-start | bytes 589832 | tf_op jit(solution)/shard_map/ppermute | solution.py:186
  70.2 3.0 %product.1 = bf16[8,48,128]{2,1,0:T(8,128)(2,1)} custom-call(s32[8]{0:T(128)} %stack.69.index_ref, bf16[96,256]{1,0:T(8,128)(2,1)} %copy-done.1, bf16[96,256]{1,0:T(8,128)(2,1)} %copy-done.4, bf16[96,256]{1,0:T(8,128)(2,1)} %copy-done.3, bf16[96,256]{1,0:T(8,128)(2,1)} %copy-done.2, bf16[96,256]{1,0:T(8,128)(2,1)} %get-tuple-element.14.refs_4_, ...), custom_call_target="tpu_custom_call" | custom-call | tf_op jit(solution)/shard_map/product/pallas_call | solution.py:157
  73.3 10.9 %all_to_all.5.shares_ref = bf16[8,48,128]{2,1,0:T(8,128)(2,1)} all-to-all(bf16[8,48,128]{2,1,0:T(8,128)(2,1)} %product.1), channel_id=1, replica_groups=mesh['zh'=4,'x'=4,'core'=2,'y'=4,'zl'=2] {'y','zl'}, dimensions={0} | all-to-all | bytes 196608 | tf_op jit(solution)/shard_map/all_to_all | solution.py:224
  84.2 1.6 %finish.1 = f32[96,64]{1,0:T(8,128)} custom-call(bf16[8,48,128]{2,1,0:T(8,128)(2,1)} %all_to_all.5.shares_ref), custom_call_target="tpu_custom_call" | custom-call | tf_op jit(solution)/shard_map/finish/pallas_call | solution.py:177
  85.8 1.5 %copy.5 = f32[96,64]{0,1:T(8,128)} copy(f32[96,64]{1,0:T(8,128)} %finish.1) | data formatting | bytes 49152 | tf_op jit(solution)/shard_map/finish/pallas_call | solution.py:177
  (28 shorter events, 5.3 us)
Async XLA Ops:
  14.4 5.0 %collective-permute-start = (f32[96,1024]{1,0:T(8,128)}, f32[96,1024]{1,0:T(8,128)S(1)}, u32[]{:S(2)}, u32[]{:S(2)}) collective-permute-start(f32[96,1024]{1,0:T(8,128)} %pull.5), channel_id=1, source_target_pairs={{0,8},{8,0},{1,9},{9,1},{2,10},{10,2},{3,11},{11,3},{4,12},{12,4},... | collective-permute-start | bytes 1179656 | tf_op jit(solution)/shard_map/ppermute | solution.py:186
  19.4 0.8 copy-start
  25.1 19.1 %collective-permute-start.1 = (f32[96,256]{1,0:T(8,128)}, f32[96,256]{1,0:T(8,128)S(1)}, u32[]{:S(2)}, u32[]{:S(2)}) collective-permute-start(f32[96,256]{1,0:T(8,128)} %pull.7), channel_id=1, source_target_pairs={{0,32},{16,48},{32,0},{48,16},{1,33},{17,49},{33,1},{49,17},{2,34}... | collective-permute-start | bytes 294920 | tf_op jit(solution)/shard_map/ppermute | solution.py:186
  31.1 13.2 %collective-permute-start.2 = (f32[96,256]{1,0:T(8,128)}, f32[96,256]{1,0:T(8,128)S(1)}, u32[]{:S(2)}, u32[]{:S(2)}) collective-permute-start(f32[96,256]{1,0:T(8,128)} %pull.8), channel_id=1, source_target_pairs={{0,16},{16,32},{32,48},{48,0},{1,17},{17,33},{33,49},{49,1},{2,18}... | collective-permute-start | bytes 294920 | tf_op jit(solution)/shard_map/ppermute | solution.py:186
  36.3 8.0 %collective-permute-start.3 = (f32[96,256]{1,0:T(8,128)}, f32[96,256]{1,0:T(8,128)S(1)}, u32[]{:S(2)}, u32[]{:S(2)}) collective-permute-start(f32[96,256]{1,0:T(8,128)} %pull.9), channel_id=1, source_target_pairs={{0,48},{16,0},{32,16},{48,32},{1,49},{17,1},{33,17},{49,33},{2,50}... | collective-permute-start | bytes 294920 | tf_op jit(solution)/shard_map/ppermute | solution.py:186
  45.2 9.4 %collective-permute-start.6 = (bf16[96,256]{1,0:T(8,128)(2,1)S(1)}, bf16[96,256]{1,0:T(8,128)(2,1)S(1)}, u32[]{:S(2)}, u32[]{:S(2)}) collective-permute-start(bf16[96,256]{1,0:T(8,128)(2,1)S(1)} %get-tuple-element.9), channel_id=1, source_target_pairs={{0,192},{64,0},{128,64},{192,128},{1,193},{65,1},{129,65},{193,129... | collective-permute-start | bytes 147464 | tf_op jit(solution)/shard_map/ppermute | solution.py:186
  51.3 5.1 %collective-permute-start.5 = (bf16[96,256]{1,0:T(8,128)(2,1)S(1)}, bf16[96,256]{1,0:T(8,128)(2,1)S(1)}, u32[]{:S(2)}, u32[]{:S(2)}) collective-permute-start(bf16[96,256]{1,0:T(8,128)(2,1)S(1)} %get-tuple-element.9), channel_id=1, source_target_pairs={{0,64},{64,128},{128,192},{192,0},{1,65},{65,129},{129,193},{193,1... | collective-permute-start | bytes 147464 | tf_op jit(solution)/shard_map/ppermute | solution.py:186
  51.3 7.1 %collective-permute-start.4 = (bf16[96,256]{1,0:T(8,128)(2,1)S(1)}, bf16[96,256]{1,0:T(8,128)(2,1)S(1)}, u32[]{:S(2)}, u32[]{:S(2)}) collective-permute-start(bf16[96,256]{1,0:T(8,128)(2,1)S(1)} %get-tuple-element.9), channel_id=1, source_target_pairs={{0,128},{64,192},{128,0},{192,64},{1,129},{65,193},{129,1},{193,65... | collective-permute-start | bytes 147464 | tf_op jit(solution)/shard_map/ppermute | solution.py:186
  58.4 11.8 %copy-start.1 = (bf16[96,256]{1,0:T(8,128)(2,1)}, bf16[96,256]{1,0:T(8,128)(2,1)S(1)}, u32[]{:S(2)}) copy-start(bf16[96,256]{1,0:T(8,128)(2,1)S(1)} %add_convert_fusion.refs_0_) | copy-start | bytes 147460
  58.4 3.0 %collective-permute-start.9 = (bf16[96,256]{1,0:T(8,128)(2,1)S(1)}, bf16[96,256]{1,0:T(8,128)(2,1)S(1)}, u32[]{:S(2)}, u32[]{:S(2)}) collective-permute-start(bf16[96,256]{1,0:T(8,128)(2,1)S(1)} %add_convert_fusion.refs_0_), channel_id=1, source_target_pairs={{0,48},{16,0},{32,16},{48,32},{1,49},{17,1},{33,17},{49,33},{2,50}... | collective-permute-start | bytes 147464 | tf_op jit(solution)/shard_map/ppermute | solution.py:186
  58.6 4.2 %collective-permute-start.8 = (bf16[96,256]{1,0:T(8,128)(2,1)S(1)}, bf16[96,256]{1,0:T(8,128)(2,1)S(1)}, u32[]{:S(2)}, u32[]{:S(2)}) collective-permute-start(bf16[96,256]{1,0:T(8,128)(2,1)S(1)} %add_convert_fusion.refs_0_), channel_id=1, source_target_pairs={{0,16},{16,32},{32,48},{48,0},{1,17},{17,33},{33,49},{49,1},{2,18}... | collective-permute-start | bytes 147464 | tf_op jit(solution)/shard_map/ppermute | solution.py:186
  59.9 4.6 %collective-permute-start.7 = (bf16[96,256]{1,0:T(8,128)(2,1)S(1)}, bf16[96,256]{1,0:T(8,128)(2,1)S(1)}, u32[]{:S(2)}, u32[]{:S(2)}) collective-permute-start(bf16[96,256]{1,0:T(8,128)(2,1)S(1)} %add_convert_fusion.refs_0_), channel_id=1, source_target_pairs={{0,32},{16,48},{32,0},{48,16},{1,33},{17,49},{33,1},{49,17},{2,34}... | collective-permute-start | bytes 147464 | tf_op jit(solution)/shard_map/ppermute | solution.py:186
  61.4 8.8 %copy-start.2 = (bf16[96,256]{1,0:T(8,128)(2,1)}, bf16[96,256]{1,0:T(8,128)(2,1)S(1)}, u32[]{:S(2)}) copy-start(bf16[96,256]{1,0:T(8,128)(2,1)S(1)} %collective-permute-done.9.refs_3_) | copy-start | bytes 147460
  62.8 7.4 %copy-start.3 = (bf16[96,256]{1,0:T(8,128)(2,1)}, bf16[96,256]{1,0:T(8,128)(2,1)S(1)}, u32[]{:S(2)}) copy-start(bf16[96,256]{1,0:T(8,128)(2,1)S(1)} %collective-permute-done.8.refs_2_) | copy-start | bytes 147460
  64.6 5.7 %copy-start.4 = (bf16[96,256]{1,0:T(8,128)(2,1)}, bf16[96,256]{1,0:T(8,128)(2,1)S(1)}, u32[]{:S(2)}) copy-start(bf16[96,256]{1,0:T(8,128)(2,1)S(1)} %collective-permute-done.7.refs_1_) | copy-start | bytes 147460
  64.6 5.0 %collective-permute-start.10 = (bf16[96,1024]{1,0:T(8,128)(2,1)S(1)}, bf16[96,1024]{1,0:T(8,128)(2,1)S(1)}, u32[]{:S(2)}, u32[]{:S(2)}) collective-permute-start(bf16[96,1024]{1,0:T(8,128)(2,1)S(1)} %pad_maximum_fusion), channel_id=1, source_target_pairs={{0,8},{8,0},{1,9},{9,1},{2,10},{10,2},{3,11},{11,3},{4,12},{12,4},... | collective-permute-start | bytes 589832 | tf_op jit(solution)/shard_map/ppermute | solution.py:186

commit v2 on v1

v2 whole, which is shorter than its diff:
```python
import functools

import jax
import jax.numpy as jnp
from jax import lax
from jax.experimental import pallas as pl
from jax.experimental.pallas import tpu as pltpu
from jax.sharding import Mesh, PartitionSpec as P

support_radius = 0.12
stretch = 4.0 / support_radius
depth = 128
span = 256
whole = pl.BlockSpec(memory_space=pltpu.VMEM)
params = pltpu.CompilerParams(vmem_limit_bytes=16 * 1024 * 1024)


def pieces_of(values):
    high = values.astype(jnp.bfloat16).astype(jnp.float32)
    rest = values - high
    middle = rest.astype(jnp.bfloat16).astype(jnp.float32)
    low = (rest - middle).astype(jnp.bfloat16).astype(jnp.float32)
    return high, middle, low


def write_features(xyz_ref, rows, is_node):
    count = xyz_ref.shape[1]
    place = (xyz_ref[...] - 0.5) * stretch
    norm = (
        place[0:1] * place[0:1] + place[1:2] * place[1:2] + place[2:3] * place[2:3]
    )
    parts = pieces_of(place)
    norm_parts = pieces_of(norm)
    ones = jnp.ones((3, count), jnp.float32)
    rows[...] = jnp.zeros_like(rows)
    for i in range(3):
        for j in range(3):
            k = 3 * (3 * i + j)
            rows[k : k + 3, :] = parts[i] if is_node else -2.0 * parts[j]
    norm_at, ones_at = (27, 30) if is_node else (30, 27)
    rows[ones_at : ones_at + 3, :] = ones
    for i in range(3):
        rows[norm_at + i : norm_at + i + 1, :] = norm_parts[i]


def features_kernel(node_ref, ctrl_ref, node_out, ctrl_out, node_rows, ctrl_rows):
    write_features(node_ref, node_rows, True)
    write_features(ctrl_ref, ctrl_rows, False)
    ctrl_out[...] = ctrl_rows[...].astype(jnp.bfloat16)
    node_out[...] = node_rows[...].T.astype(jnp.bfloat16)


def features(node_xyz, ctrl_xyz):
    nodes, ctrls = node_xyz.shape[1], ctrl_xyz.shape[1]
    return pl.pallas_call(
        features_kernel,
        out_shape=[
            jax.ShapeDtypeStruct((nodes, depth), jnp.bfloat16),
            jax.ShapeDtypeStruct((depth, ctrls), jnp.bfloat16),
        ],
        scratch_shapes=[
            pltpu.VMEM((depth, nodes), jnp.float32),
            pltpu.VMEM((depth, ctrls), jnp.float32),
        ],
        cost_estimate=pl.CostEstimate(
            flops=nodes * 1000, bytes_accessed=nodes * 512, transcendentals=0
        ),
        in_specs=[whole] * 2,
        out_specs=[whole] * 2,
        compiler_params=params,
        name="features",
    )(node_xyz, ctrl_xyz)


def wendland(squared):
    squared = jnp.maximum(squared, 1e-30)
    r4 = squared * lax.rsqrt(squared)
    remain = jnp.maximum(4.0 - r4, 0.0)
    remain2 = remain * remain
    return (remain2 * remain2 * (r4 + 1.0)).astype(jnp.bfloat16)


def pull_kernel(tile, other, first, blocks, add_at, *refs):
    node_ref, ctrl_ref, sens_ref, out_ref = refs[0], refs[1], refs[2], refs[-1]
    nodes = node_ref.shape[0]
    core = lax.axis_index("core")
    x = lax.axis_index("x")
    half = (1 - core) if other else core
    for j in range(blocks):
        quarter = lax.rem(x + first + j, 4)
        from_column = pl.multiple_of((half * 4 + quarter) * span, span)
        weights = ctrl_ref[:, pl.ds(from_column, span)]

        def body(i, acc):
            at = pl.multiple_of(i * tile, tile)
            squared = jnp.dot(
                node_ref[pl.ds(at, tile), :],
                weights,
                preferred_element_type=jnp.float32,
            )
            return acc + jnp.dot(
                sens_ref[:, pl.ds(at, tile)],
                wendland(squared),
                preferred_element_type=jnp.float32,
            )

        acc = lax.fori_loop(
            0, nodes // tile, body, jnp.zeros((out_ref.shape[0], span), jnp.float32)
        )
        acc = acc * (1.0 / 256.0)
        if len(refs) == 5:
            acc = acc + refs[3][:, add_at * span : (add_at + 1) * span]
        out_ref[:, j * span : (j + 1) * span] = acc


def pull(
    other, first, blocks, node_feat, ctrl_feat, sens, add=None, add_at=0, tile=2048
):
    nodes = node_feat.shape[0]
    rows = sens.shape[0]
    args = [node_feat, ctrl_feat, sens] + ([] if add is None else [add])
    return pl.pallas_call(
        functools.partial(pull_kernel, tile, other, first, blocks, add_at),
        out_shape=jax.ShapeDtypeStruct((rows, blocks * span), jnp.float32),
        in_specs=[whole] * len(args),
        out_specs=whole,
        cost_estimate=pl.CostEstimate(
            flops=blocks * span * nodes * 400,
            bytes_accessed=nodes * 448,
            transcendentals=blocks * span * nodes,
        ),
        compiler_params=params,
        name="pull",
    )(*args)


def product_kernel(order, *refs):
    blocks, inverse_ref, out_ref = refs[:-2], refs[-2], refs[-1]
    core = lax.axis_index("core")
    x = lax.axis_index("x")
    total = None
    for half, joined in ((core, blocks[:-1]), (1 - core, blocks[-1:])):
        for i, by in enumerate(order):
            at = pl.multiple_of((half * 4 + lax.rem(x + 4 - by, 4)) * span, span)
            if len(joined) == 1:
                block = joined[0][:, i * span : (i + 1) * span]
            else:
                block = joined[i][...]
            term = jnp.dot(
                block,
                inverse_ref[pl.ds(at, span), :],
                preferred_element_type=jnp.float32,
            )
            total = term if total is None else total + term
    shares, rows, lanes = out_ref.shape
    width = lanes // 2
    for j in range(shares):
        share = total[:, j * width : (j + 1) * width]
        out_ref[j] = jnp.concatenate([share[:rows], share[rows:]], axis=1).astype(
            out_ref.dtype
        )


def product(order, blocks, inverse, shares):
    rows, width = blocks[0].shape[0], inverse.shape[1] // shares
    return pl.pallas_call(
        functools.partial(product_kernel, order),
        out_shape=jax.ShapeDtypeStruct((shares, rows // 2, 2 * width), jnp.bfloat16),
        in_specs=[whole] * (len(blocks) + 1),
        out_specs=whole,
        compiler_params=params,
        name="product",
    )(*blocks, inverse)


def finish_kernel(shares_ref, out_ref):
    total = shares_ref[0].astype(jnp.float32)
    for j in range(1, shares_ref.shape[0]):
        total = total + shares_ref[j].astype(jnp.float32)
    rows, lanes = total.shape
    turned = total.T
    out_ref[:, 0:rows] = turned[: lanes // 2]
    out_ref[:, rows:] = turned[lanes // 2 :]


def finish(shares):
    _, rows, lanes = shares.shape
    return pl.pallas_call(
        finish_kernel,
        out_shape=jax.ShapeDtypeStruct((lanes // 2, 2 * rows), jnp.float32),
        in_specs=[whole],
        out_specs=whole,
        compiler_params=params,
        name="finish",
    )(shares).T


def shifted(value, axis, by):
    size = lax.axis_size(axis)
    return lax.ppermute(value, axis, [(i, (i + by) % size) for i in range(size)])


def per_device(sensitivity, node_xyz, ctrl_xyz, inverse):
    node_feat, ctrl_feat = features(node_xyz, ctrl_xyz)
    pulled = functools.partial(
        pull, node_feat=node_feat, ctrl_feat=ctrl_feat, sens=sensitivity
    )
    sent_on = shifted(pulled(True, 1, 3), "core", 1)
    kept = shifted(pulled(True, 0, 1), "core", 1)
    order = (2, 1, 3)
    arrived = [
        shifted(pulled(False, by, 1, add=sent_on, add_at=by - 1), "x", by)
        for by in order
    ]
    summed = pulled(False, 0, 1, add=kept)
    for part in arrived:
        summed = summed + part

    low = summed.astype(jnp.bfloat16)
    for by in order:
        summed = summed + shifted(low, "zh", by).astype(jnp.float32)
    mine = summed.astype(jnp.bfloat16)

    along_x = [mine] + [shifted(mine, "x", by) for by in order]
    swapped = shifted(jnp.concatenate(along_x, axis=1), "core", 1)
    shares = product((0,) + order, along_x + [swapped], inverse, 8)
    arrived_shares = lax.all_to_all(
        shares, ("y", "zl"), split_axis=0, concat_axis=0, tiled=True
    )
    return finish(arrived_shares)


def solution(mesh):
    fine = Mesh(
        mesh.devices.reshape(4, 4, 2, 4, 2), ("zh", "x", "core", "y", "zl")
    )
    node, ctrl = ("zh", "x", "core"), ("y", "zl")
    in_specs = (P(None, node), P(None, node), P(None, ctrl), P(ctrl, node))
    out_specs = P(None, node + ctrl)
    return jax.shard_map(
        per_device, mesh=fine, in_specs=in_specs, out_specs=out_specs, check_vma=False
    )
```

time: 87.8 us -> 65.7 us (0.75)
  Pallas kernels: 38.2 us -> 19.1 us
  other arithmetic: 3.92 us -> 0.07 us
  starting transfers between devices: 21.7 us -> 25.5 us
  waiting for transfers between devices: 8.93 us -> 7.55 us
    pallas_call x7 -> x8, Pallas kernels: 35.8 us -> 18.5 us  [the longest x6 17.2 us: pull(): pl.pallas_call(functools.partial(pull_kernel, tile, other, first, blocks,...]
    ppermute x11 -> x12, starting transfers between devices: 21.7 us -> 25.5 us  [shifted(): lax.ppermute(value, axis, [(i, (i + by) % size) for i in range(size)])]
    another operation x4 -> x0, other arithmetic: 2.45 us -> none  [quarter(): index = jnp.stack([own + which, which])]
    unnamed x10 -> x8, local copies, waits for them, and re-layouts: 0.78 us -> 2.73 us
    pallas_call x1, Pallas kernels: 2.49 us -> 0.59 us  [features(): pl.pallas_call(features_kernel, out_shape=[jax.ShapeDtypeStruct((nodes, d...]
    pallas_call x1 -> x0, local copies, waits for them, and re-layouts: 1.49 us -> none  [finish(): pl.pallas_call(finish_kernel, out_shape=jax.ShapeDtypeStruct((2 * rows, l...]
    ppermute x11 -> x12, waiting for transfers between devices: 8.93 us -> 7.55 us  [shifted(): lax.ppermute(value, axis, [(i, (i + by) % size) for i in range(size)])]
    convert_element_type x1, other arithmetic: 0.92 us -> 0.03 us  [per_device(): low = summed.astype(jnp.bfloat16)]
  transfers between devices with their start and end apart: 11 -> 12, of which waited for: 6 -> 6; matrix products, arithmetic and copies ran while one was open for 3% -> 0% of each run, Pallas kernels for 17% -> 16%
where the time goes in v2:
time: 65.7 us; the launch traced here: 65.5 us
  starting transfers between devices  25.5 us (39%)
  Pallas kernels  19.1 us (29%)
  blocking collectives  10.3 us (16%)
  waiting for transfers between devices  7.55 us (11%)
  local copies, waits for them, and re-layouts  2.73 us (4%)
    ppermute x12, starting transfers between devices, shifted(): lax.ppermute(value, axis, [(i, (i + by) % size) for i in range(size)])  25.5 us
    pallas_call x6, Pallas kernels, pull(): pl.pallas_call(functools.partial(pull_kernel, tile, other, first, blocks,...  17.2 us
    all_to_all x1, blocking collectives, per_device(): lax.all_to_all(shares, ('y', 'zl'), split_axis=0, concat_axis=0, tiled=True)  10.3 us
    ppermute x12, waiting for transfers between devices, shifted(): lax.ppermute(value, axis, [(i, (i + by) % size) for i in range(size)])  7.55 us
    unnamed x8, local copies, waits for them, and re-layouts  2.73 us
  transfers between devices with their start and end apart: 12, of which 6 were waited for; matrix products, arithmetic and copies ran while one was open for 0% of the time, Pallas kernels for 16%

profile of v2, /device:TPU:1, one launch (start us, length us, event | category | flops | bytes accessed | tf_op | source)
XLA Modules:
  0.0 65.5 jit_solution(6733900228613866114)
XLA Ops:
  0.0 0.8 %copy-done.2 = f32[3,4096]{1,0:T(4,128)S(1)} copy-done((f32[3,4096]{1,0:T(4,128)S(1)}, f32[3,4096]{1,0:T(4,128)}, u32[]{:S(2)}) %copy-start.2) | copy-done | bytes 49176
  0.8 0.8 %copy-done.3 = f32[3,2048]{1,0:T(4,128)S(1)} copy-done((f32[3,2048]{1,0:T(4,128)S(1)}, f32[3,2048]{1,0:T(4,128)}, u32[]{:S(2)}) %copy-start.3) | copy-done | bytes 24600
  1.6 0.6 features.1
  2.2 1.1 %copy-done = bf16[96,4096]{1,0:T(8,128)(2,1)S(1)} copy-done((bf16[96,4096]{1,0:T(8,128)(2,1)S(1)}, bf16[96,4096]{1,0:T(8,128)(2,1)}, u32[]{:S(2)}) %copy-start) | copy-done | bytes 786456
  3.3 6.4 %pull.8 = f32[96,768]{1,0:T(8,128)S(1)} custom-call(bf16[4096,128]{1,0:T(8,128)(2,1)S(1)} %get-tuple-element.7.refs_0_, bf16[128,2048]{1,0:T(8,128)(2,1)S(1)} %get-tuple-element.8.refs_1_, bf16[96,4096]{1,0:T(8,128)(2,1)S(1)} %copy-done), custom_call_target="tpu_custom_call" | custom-call | flops 1258291200 | bytes 1835008 | tf_op jit(solution)/shard_map/pull/pallas_call | solution.py:122
  9.8 3.3 %collective-permute-start.1 = (f32[96,768]{1,0:T(8,128)S(1)}, f32[96,768]{1,0:T(8,128)S(1)}, u32[]{:S(2)}, u32[]{:S(2)}) collective-permute-start(f32[96,768]{1,0:T(8,128)S(1)} %pull.8), channel_id=1, source_target_pairs={{0,8},{8,0},{1,9},{9,1},{2,10},{10,2},{3,11},{11,3},{4,12},{12,4},... | collective-permute-start | bytes 884744 | tf_op jit(solution)/shard_map/ppermute | solution.py:200
  13.1 2.1 %pull.6 = f32[96,256]{1,0:T(8,128)S(1)} custom-call(bf16[4096,128]{1,0:T(8,128)(2,1)S(1)} %get-tuple-element.7.refs_0_, bf16[128,2048]{1,0:T(8,128)(2,1)S(1)} %get-tuple-element.8.refs_1_, bf16[96,4096]{1,0:T(8,128)(2,1)S(1)} %copy-done), custom_call_target="tpu_custom_call" | custom-call | flops 419430400 | bytes 1835008 | tf_op jit(solution)/shard_map/pull/pallas_call | solution.py:122
  15.3 2.2 %pull.9 = f32[96,256]{1,0:T(8,128)S(1)} custom-call(bf16[4096,128]{1,0:T(8,128)(2,1)S(1)} %get-tuple-element.7.refs_0_, bf16[128,2048]{1,0:T(8,128)(2,1)S(1)} %get-tuple-element.8.refs_1_, bf16[96,4096]{1,0:T(8,128)(2,1)S(1)} %copy-done, f32[96,768]{1,0:T(8,128)S(1)} %collective-permute-done.1.refs_3_), custom_call_target="tpu_custom_call" | custom-call | flops 419430400 | bytes 1835008 | tf_op jit(solution)/shard_map/pull/pallas_call | solution.py:122
  17.5 1.1 %collective-permute-start.2 = (f32[96,256]{1,0:T(8,128)S(1)}, f32[96,256]{1,0:T(8,128)S(1)}, u32[]{:S(2)}, u32[]{:S(2)}) collective-permute-start(f32[96,256]{1,0:T(8,128)S(1)} %pull.9), channel_id=1, source_target_pairs={{0,32},{16,48},{32,0},{48,16},{1,33},{17,49},{33,1},{49,17},{2,34}... | collective-permute-start | bytes 294920 | tf_op jit(solution)/shard_map/ppermute | solution.py:200
  18.6 2.2 %pull.10 = f32[96,256]{1,0:T(8,128)S(1)} custom-call(bf16[4096,128]{1,0:T(8,128)(2,1)S(1)} %get-tuple-element.7.refs_0_, bf16[128,2048]{1,0:T(8,128)(2,1)S(1)} %get-tuple-element.8.refs_1_, bf16[96,4096]{1,0:T(8,128)(2,1)S(1)} %copy-done, f32[96,768]{1,0:T(8,128)S(1)} %collective-permute-done.1.refs_3_), custom_call_target="tpu_custom_call" | custom-call | flops 419430400 | bytes 1835008 | tf_op jit(solution)/shard_map/pull/pallas_call | solution.py:122
  21.2 2.1 %pull.11 = f32[96,256]{1,0:T(8,128)S(1)} custom-call(bf16[4096,128]{1,0:T(8,128)(2,1)S(1)} %get-tuple-element.7.refs_0_, bf16[128,2048]{1,0:T(8,128)(2,1)S(1)} %get-tuple-element.8.refs_1_, bf16[96,4096]{1,0:T(8,128)(2,1)S(1)} %copy-done, f32[96,768]{1,0:T(8,128)S(1)} %collective-permute-done.1.refs_3_), custom_call_target="tpu_custom_call" | custom-call | flops 419430400 | bytes 1835008 | tf_op jit(solution)/shard_map/pull/pallas_call | solution.py:122
  23.3 2.4 %collective-permute-start.4 = (f32[96,256]{1,0:T(8,128)S(1)}, f32[96,256]{1,0:T(8,128)S(1)}, u32[]{:S(2)}, u32[]{:S(2)}) collective-permute-start(f32[96,256]{1,0:T(8,128)S(1)} %pull.11), channel_id=1, source_target_pairs={{0,48},{16,0},{32,16},{48,32},{1,49},{17,1},{33,17},{49,33},{2,50}... | collective-permute-start | bytes 294920 | tf_op jit(solution)/shard_map/ppermute | solution.py:200
  25.8 2.2 %pull.7 = f32[96,256]{1,0:T(8,128)S(1)} custom-call(bf16[4096,128]{1,0:T(8,128)(2,1)S(1)} %get-tuple-element.7.refs_0_, bf16[128,2048]{1,0:T(8,128)(2,1)S(1)} %get-tuple-element.8.refs_1_, bf16[96,4096]{1,0:T(8,128)(2,1)S(1)} %copy-done, f32[96,256]{1,0:T(8,128)S(1)} %collective-permute-done.refs_3_), custom_call_target="tpu_custom_call" | custom-call | flops 419430400 | bytes 1835008 | tf_op jit(solution)/shard_map/pull/pallas_call | solution.py:122
  28.0 7.0 %collective-permute-start.5 = (bf16[96,256]{1,0:T(8,128)(2,1)S(1)}, bf16[96,256]{1,0:T(8,128)(2,1)S(1)}, u32[]{:S(2)}, u32[]{:S(2)}) collective-permute-start(bf16[96,256]{1,0:T(8,128)(2,1)S(1)} %get-tuple-element.9), channel_id=1, source_target_pairs={{0,128},{64,192},{128,0},{192,64},{1,129},{65,193},{129,1},{193,65... | collective-permute-start | bytes 147464 | tf_op jit(solution)/shard_map/ppermute | solution.py:200
  35.0 1.2 %collective-permute-start.6 = (bf16[96,256]{1,0:T(8,128)(2,1)S(1)}, bf16[96,256]{1,0:T(8,128)(2,1)S(1)}, u32[]{:S(2)}, u32[]{:S(2)}) collective-permute-start(bf16[96,256]{1,0:T(8,128)(2,1)S(1)} %get-tuple-element.9), channel_id=1, source_target_pairs={{0,64},{64,128},{128,192},{192,0},{1,65},{65,129},{129,193},{193,1... | collective-permute-start | bytes 147464 | tf_op jit(solution)/shard_map/ppermute | solution.py:200
  36.2 2.4 %collective-permute-start.7 = (bf16[96,256]{1,0:T(8,128)(2,1)S(1)}, bf16[96,256]{1,0:T(8,128)(2,1)S(1)}, u32[]{:S(2)}, u32[]{:S(2)}) collective-permute-start(bf16[96,256]{1,0:T(8,128)(2,1)S(1)} %get-tuple-element.9), channel_id=1, source_target_pairs={{0,192},{64,0},{128,64},{192,128},{1,193},{65,1},{129,65},{193,129... | collective-permute-start | bytes 147464 | tf_op jit(solution)/shard_map/ppermute | solution.py:200
  38.6 1.9 %collective-permute-done.6 = bf16[96,256]{1,0:T(8,128)(2,1)S(1)} collective-permute-done((bf16[96,256]{1,0:T(8,128)(2,1)S(1)}, bf16[96,256]{1,0:T(8,128)(2,1)S(1)}, u32[]{:S(2)}, u32[]{:S(2)}) %collective-permute-start.6) | collective-permute-done | bytes 49184 | tf_op jit(solution)/shard_map/ppermute | solution.py:200
  41.1 2.2 %collective-permute-start.10 = (bf16[96,256]{1,0:T(8,128)(2,1)S(1)}, bf16[96,256]{1,0:T(8,128)(2,1)S(1)}, u32[]{:S(2)}, u32[]{:S(2)}) collective-permute-start(bf16[96,256]{1,0:T(8,128)(2,1)S(1)} %add_convert_fusion.refs_0_), channel_id=1, source_target_pairs={{0,48},{16,0},{32,16},{48,32},{1,49},{17,1},{33,17},{49,33},{2,50}... | collective-permute-start | bytes 147464 | tf_op jit(solution)/shard_map/ppermute | solution.py:200
  43.2 0.7 %collective-permute-start.9 = (bf16[96,256]{1,0:T(8,128)(2,1)S(1)}, bf16[96,256]{1,0:T(8,128)(2,1)S(1)}, u32[]{:S(2)}, u32[]{:S(2)}) collective-permute-start(bf16[96,256]{1,0:T(8,128)(2,1)S(1)} %add_convert_fusion.refs_0_), channel_id=1, source_target_pairs={{0,16},{16,32},{32,48},{48,0},{1,17},{17,33},{33,49},{49,1},{2,18}... | collective-permute-start | bytes 147464 | tf_op jit(solution)/shard_map/ppermute | solution.py:200
  44.4 3.4 %collective-permute-done.8.refs_1_ = bf16[96,256]{1,0:T(8,128)(2,1)S(1)} collective-permute-done((bf16[96,256]{1,0:T(8,128)(2,1)S(1)}, bf16[96,256]{1,0:T(8,128)(2,1)S(1)}, u32[]{:S(2)}, u32[]{:S(2)}) %collective-permute-start.8) | collective-permute-done | bytes 49184 | tf_op jit(solution)/shard_map/ppermute | solution.py:200
  47.9 4.8 %collective-permute-start.11 = (bf16[96,1024]{1,0:T(8,128)(2,1)S(1)}, bf16[96,1024]{1,0:T(8,128)(2,1)S(1)}, u32[]{:S(2)}, u32[]{:S(2)}) collective-permute-start(bf16[96,1024]{1,0:T(8,128)(2,1)S(1)} %pad_maximum_fusion), channel_id=1, source_target_pairs={{0,8},{8,0},{1,9},{9,1},{2,10},{10,2},{3,11},{11,3},{4,12},{12,4},... | collective-permute-start | bytes 589832 | tf_op jit(solution)/shard_map/ppermute | solution.py:200
  52.7 1.1 %collective-permute-done.11.refs_4_ = bf16[96,1024]{1,0:T(8,128)(2,1)S(1)} collective-permute-done((bf16[96,1024]{1,0:T(8,128)(2,1)S(1)}, bf16[96,1024]{1,0:T(8,128)(2,1)S(1)}, u32[]{:S(2)}, u32[]{:S(2)}) %collective-permute-start.11) | collective-permute-done | bytes 196640 | tf_op jit(solution)/shard_map/ppermute | solution.py:200
  54.4 10.3 %all_to_all.5.shares_ref = bf16[8,48,128]{2,1,0:T(8,128)(2,1)S(1)} all-to-all(bf16[8,48,128]{2,1,0:T(8,128)(2,1)S(1)} %product.1), channel_id=1, replica_groups=mesh['zh'=4,'x'=4,'core'=2,'y'=4,'zl'=2] {'y','zl'}, dimensions={0} | all-to-all | bytes 196608 | tf_op jit(solution)/shard_map/all_to_all | solution.py:227
  64.7 0.8 %finish.1 = f32[64,96]{1,0:T(8,128)} custom-call(bf16[8,48,128]{2,1,0:T(8,128)(2,1)S(1)} %all_to_all.5.shares_ref), custom_call_target="tpu_custom_call" | custom-call | tf_op jit(solution)/shard_map/finish/pallas_call | solution.py:188
  (21 shorter events, 2.3 us)
Async XLA Ops:
  0.0 0.8 %copy-start.2 = (f32[3,4096]{1,0:T(4,128)S(1)}, f32[3,4096]{1,0:T(4,128)}, u32[]{:S(2)}) copy-start(f32[3,4096]{1,0:T(4,128)} %node_ref.1) | copy-start | bytes 147460
  0.8 0.8 %copy-start.3 = (f32[3,2048]{1,0:T(4,128)S(1)}, f32[3,2048]{1,0:T(4,128)}, u32[]{:S(2)}) copy-start(f32[3,2048]{1,0:T(4,128)} %ctrl_ref.1) | copy-start | bytes 73732
  2.2 1.1 %copy-start = (bf16[96,4096]{1,0:T(8,128)(2,1)S(1)}, bf16[96,4096]{1,0:T(8,128)(2,1)}, u32[]{:S(2)}) copy-start(bf16[96,4096]{1,0:T(8,128)(2,1)} %refs_2_.11) | copy-start | bytes 2359300
  9.8 5.5 %collective-permute-start.1 = (f32[96,768]{1,0:T(8,128)S(1)}, f32[96,768]{1,0:T(8,128)S(1)}, u32[]{:S(2)}, u32[]{:S(2)}) collective-permute-start(f32[96,768]{1,0:T(8,128)S(1)} %pull.8), channel_id=1, source_target_pairs={{0,8},{8,0},{1,9},{9,1},{2,10},{10,2},{3,11},{11,3},{4,12},{12,4},... | collective-permute-start | bytes 884744 | tf_op jit(solution)/shard_map/ppermute | solution.py:200
  15.2 10.6 %collective-permute-start = (f32[96,256]{1,0:T(8,128)S(1)}, f32[96,256]{1,0:T(8,128)S(1)}, u32[]{:S(2)}, u32[]{:S(2)}) collective-permute-start(f32[96,256]{1,0:T(8,128)S(1)} %pull.6), channel_id=1, source_target_pairs={{0,8},{8,0},{1,9},{9,1},{2,10},{10,2},{3,11},{11,3},{4,12},{12,4},... | collective-permute-start | bytes 294920 | tf_op jit(solution)/shard_map/ppermute | solution.py:200
  17.5 10.4 %collective-permute-start.2 = (f32[96,256]{1,0:T(8,128)S(1)}, f32[96,256]{1,0:T(8,128)S(1)}, u32[]{:S(2)}, u32[]{:S(2)}) collective-permute-start(f32[96,256]{1,0:T(8,128)S(1)} %pull.9), channel_id=1, source_target_pairs={{0,32},{16,48},{32,0},{48,16},{1,33},{17,49},{33,1},{49,17},{2,34}... | collective-permute-start | bytes 294920 | tf_op jit(solution)/shard_map/ppermute | solution.py:200
  20.8 7.2 %collective-permute-start.3 = (f32[96,256]{1,0:T(8,128)S(1)}, f32[96,256]{1,0:T(8,128)S(1)}, u32[]{:S(2)}, u32[]{:S(2)}) collective-permute-start(f32[96,256]{1,0:T(8,128)S(1)} %pull.10), channel_id=1, source_target_pairs={{0,16},{16,32},{32,48},{48,0},{1,17},{17,33},{33,49},{49,1},{2,18}... | collective-permute-start | bytes 294920 | tf_op jit(solution)/shard_map/ppermute | solution.py:200
  23.3 30.5 %copy-start.1 = (bf16[2048,512]{1,0:T(8,128)(2,1)S(1)}, bf16[2048,512]{1,0:T(8,128)(2,1)}, u32[]{:S(2)}) copy-start(bf16[2048,512]{1,0:T(8,128)(2,1)} %refs_5_.1) | copy-start | bytes 6291460
  23.3 4.6 %collective-permute-start.4 = (f32[96,256]{1,0:T(8,128)S(1)}, f32[96,256]{1,0:T(8,128)S(1)}, u32[]{:S(2)}, u32[]{:S(2)}) collective-permute-start(f32[96,256]{1,0:T(8,128)S(1)} %pull.11), channel_id=1, source_target_pairs={{0,48},{16,0},{32,16},{48,32},{1,49},{17,1},{33,17},{49,33},{2,50}... | collective-permute-start | bytes 294920 | tf_op jit(solution)/shard_map/ppermute | solution.py:200
  28.0 10.6 %collective-permute-start.5 = (bf16[96,256]{1,0:T(8,128)(2,1)S(1)}, bf16[96,256]{1,0:T(8,128)(2,1)S(1)}, u32[]{:S(2)}, u32[]{:S(2)}) collective-permute-start(bf16[96,256]{1,0:T(8,128)(2,1)S(1)} %get-tuple-element.9), channel_id=1, source_target_pairs={{0,128},{64,192},{128,0},{192,64},{1,129},{65,193},{129,1},{193,65... | collective-permute-start | bytes 147464 | tf_op jit(solution)/shard_map/ppermute | solution.py:200
  35.0 5.5 %collective-permute-start.6 = (bf16[96,256]{1,0:T(8,128)(2,1)S(1)}, bf16[96,256]{1,0:T(8,128)(2,1)S(1)}, u32[]{:S(2)}, u32[]{:S(2)}) collective-permute-start(bf16[96,256]{1,0:T(8,128)(2,1)S(1)} %get-tuple-element.9), channel_id=1, source_target_pairs={{0,64},{64,128},{128,192},{192,0},{1,65},{65,129},{129,193},{193,1... | collective-permute-start | bytes 147464 | tf_op jit(solution)/shard_map/ppermute | solution.py:200
  36.2 4.8 %collective-permute-start.7 = (bf16[96,256]{1,0:T(8,128)(2,1)S(1)}, bf16[96,256]{1,0:T(8,128)(2,1)S(1)}, u32[]{:S(2)}, u32[]{:S(2)}) collective-permute-start(bf16[96,256]{1,0:T(8,128)(2,1)S(1)} %get-tuple-element.9), channel_id=1, source_target_pairs={{0,192},{64,0},{128,64},{192,128},{1,193},{65,1},{129,65},{193,129... | collective-permute-start | bytes 147464 | tf_op jit(solution)/shard_map/ppermute | solution.py:200
  41.1 3.3 %collective-permute-start.10 = (bf16[96,256]{1,0:T(8,128)(2,1)S(1)}, bf16[96,256]{1,0:T(8,128)(2,1)S(1)}, u32[]{:S(2)}, u32[]{:S(2)}) collective-permute-start(bf16[96,256]{1,0:T(8,128)(2,1)S(1)} %add_convert_fusion.refs_0_), channel_id=1, source_target_pairs={{0,48},{16,0},{32,16},{48,32},{1,49},{17,1},{33,17},{49,33},{2,50}... | collective-permute-start | bytes 147464 | tf_op jit(solution)/shard_map/ppermute | solution.py:200
  43.2 4.5 %collective-permute-start.8 = (bf16[96,256]{1,0:T(8,128)(2,1)S(1)}, bf16[96,256]{1,0:T(8,128)(2,1)S(1)}, u32[]{:S(2)}, u32[]{:S(2)}) collective-permute-start(bf16[96,256]{1,0:T(8,128)(2,1)S(1)} %add_convert_fusion.refs_0_), channel_id=1, source_target_pairs={{0,32},{16,48},{32,0},{48,16},{1,33},{17,49},{33,1},{49,17},{2,34}... | collective-permute-start | bytes 147464 | tf_op jit(solution)/shard_map/ppermute | solution.py:200
  43.2 4.7 %collective-permute-start.9 = (bf16[96,256]{1,0:T(8,128)(2,1)S(1)}, bf16[96,256]{1,0:T(8,128)(2,1)S(1)}, u32[]{:S(2)}, u32[]{:S(2)}) collective-permute-start(bf16[96,256]{1,0:T(8,128)(2,1)S(1)} %add_convert_fusion.refs_0_), channel_id=1, source_target_pairs={{0,16},{16,32},{32,48},{48,0},{1,17},{17,33},{33,49},{49,1},{2,18}... | collective-permute-start | bytes 147464 | tf_op jit(solution)/shard_map/ppermute | solution.py:200
  47.9 5.9 %collective-permute-start.11 = (bf16[96,1024]{1,0:T(8,128)(2,1)S(1)}, bf16[96,1024]{1,0:T(8,128)(2,1)S(1)}, u32[]{:S(2)}, u32[]{:S(2)}) collective-permute-start(bf16[96,1024]{1,0:T(8,128)(2,1)S(1)} %pad_maximum_fusion), channel_id=1, source_target_pairs={{0,8},{8,0},{1,9},{9,1},{2,10},{10,2},{3,11},{11,3},{4,12},{12,4},... | collective-permute-start | bytes 589832 | tf_op jit(solution)/shard_map/ppermute | solution.py:200
